TPU v7x, 256 devices: a whole 4x4x8 slice. The times are simulated.
256 devices in a mesh: dp: 8 (over y, core), ctx: 32 (over z, x).
Axes of the slice: x: 4, y: 4, z: 8, core: 2. Of those that a mesh axis runs over, the one named last changes fastest.
Arguments:
- normed_hidden_input: bfloat16 [8, 4096, 4096], P('dp', 'ctx'), may hold values from -6 to 6
- frozen_query_projection: bfloat16 [8, 4096, 4096], P('dp', 'ctx'), may hold values from -24 to 24
- frozen_key_projection: bfloat16 [8, 4096, 4096], P('dp', 'ctx'), may hold values from -24 to 24
- frozen_value_projection: bfloat16 [8, 4096, 4096], P('dp', 'ctx'), may hold values from -6 to 6
- cotangent: bfloat16 [8, 4096, 4096], P('dp', 'ctx'), may hold values from -0.119628906 to 0.119628906
- adapter_down_maps: bfloat16 [3, 4096, 16], replicated, may hold values from -0.09375 to 0.09375
- adapter_up_maps: bfloat16 [3, 16, 4096], replicated, may hold values from -1.5 to 1.5
- head_shift_mask: int32 [32], replicated, may hold values from 0 to 1, as said below
Outputs:
- context: bfloat16 [8, 4096, 4096], P('dp', 'ctx')
- grad_down: float32 [3, 4096, 16], replicated
- grad_up: float32 [3, 16, 4096], replicated
Inputs may be any that keep to these rules, and one draw needn't show every extreme that they name: `head_shift_mask`: exactly half of the entries are 1, the rest 0; which heads are shifted varies.
All inputs are finite; a program needn't handle non-finite values.
Results may differ from a plain program's by a relative error of at most 0.02.
The roundings to bfloat16 on the way count: a program that leaves them out, or rounds other values in their place, can miss the bound.
Values may be sent and summed in bfloat16 or wider, within the bound.
A program may use at most 64 MiB of HBM per device.

v0:
```python
import math

import jax
import jax.numpy as jnp
from jax import lax
from jax.sharding import PartitionSpec as P

HEAD_DIM = 128
GROUP = 1024
SHIFT = 512


adapter_scale = 0.25


def shift_heads(values, shift_flags, amount):
    rolled = jnp.roll(values, amount, axis=0)
    return jnp.where(shift_flags[None, :, None] == 1, rolled, values)


def group_block(segment_list):
    queries, key_rows, value_rows, grad_out = segment_list
    group_len = queries.shape[0]
    softmax_scale = 1.0 / math.sqrt(queries.shape[2])
    scores = (
        jnp.einsum("qhe,khe->hqk", queries, key_rows, preferred_element_type=jnp.float32)
        * softmax_scale
    )
    row_ids = lax.broadcasted_iota(jnp.int32, (group_len, group_len), 0)
    col_ids = lax.broadcasted_iota(jnp.int32, (group_len, group_len), 1)
    scores = jnp.where((col_ids <= row_ids)[None], scores, -1e30)
    highest = jnp.max(scores, axis=2, keepdims=True)
    exponent = jnp.exp(scores - highest)
    weights = exponent / jnp.sum(exponent, axis=2, keepdims=True)
    weights_low = weights.astype(jnp.bfloat16)
    attended = jnp.einsum(
        "hqk,khe->qhe", weights_low, value_rows, preferred_element_type=jnp.float32
    ).astype(jnp.bfloat16)
    weight_grad = jnp.einsum(
        "qhe,khe->hqk", grad_out, value_rows, preferred_element_type=jnp.float32
    )
    row_inner = jnp.sum(grad_out.astype(jnp.float32) * attended.astype(jnp.float32), axis=2)
    score_grad = weights * (weight_grad - jnp.transpose(row_inner)[:, :, None])
    score_low = score_grad.astype(jnp.bfloat16)
    query_grad = (
        jnp.einsum("hqk,khe->qhe", score_low, key_rows, preferred_element_type=jnp.float32)
        * softmax_scale
    ).astype(jnp.bfloat16)
    key_grad = (
        jnp.einsum("hqk,qhe->khe", score_low, queries, preferred_element_type=jnp.float32)
        * softmax_scale
    ).astype(jnp.bfloat16)
    value_grad = jnp.einsum(
        "hqk,qhe->khe", weights_low, grad_out, preferred_element_type=jnp.float32
    ).astype(jnp.bfloat16)
    return (attended, query_grad, key_grad, value_grad)


def attend_heads(queries, key_rows, value_rows, grad_out, shift_flags):
    total, heads, depth = queries.shape
    groups = total // GROUP

    def regroup(array):
        return shift_heads(array, shift_flags, -SHIFT).reshape(groups, GROUP, heads, depth)

    results = lax.map(
        group_block, (regroup(queries), regroup(key_rows), regroup(value_rows), regroup(grad_out))
    )
    return tuple(
        (
            shift_heads(output_part.reshape(total, heads, depth), shift_flags, SHIFT)
            for output_part in results
        )
    )


def body(
    normed_hidden_input,
    frozen_query_projection,
    frozen_key_projection,
    frozen_value_projection,
    cotangent,
    adapter_down_maps,
    adapter_up_maps,
    head_shift_mask,
):
    ctx_count = lax.axis_size("ctx")
    model_width = normed_hidden_input.shape[2]
    local_width = model_width // ctx_count
    local_heads = local_width // HEAD_DIM
    hidden_rows = normed_hidden_input[0]
    reduced_rank_rows = jnp.einsum(
        "vl,hlq->hvq", hidden_rows, adapter_down_maps, preferred_element_type=jnp.float32
    ).astype(jnp.bfloat16)
    frozen_stack = jnp.stack(
        [frozen_query_projection[0], frozen_key_projection[0], frozen_value_projection[0]]
    )
    grad_heads = lax.all_to_all(cotangent[0], "ctx", split_axis=1, concat_axis=0, tiled=True)
    local_flags = lax.dynamic_slice_in_dim(
        head_shift_mask, lax.axis_index("ctx") * local_heads, local_heads
    )
    adapter_update = jnp.einsum(
        "bsc,bci->bsi", reduced_rank_rows, adapter_up_maps, preferred_element_type=jnp.float32
    )
    projected_sequence = (frozen_stack.astype(jnp.float32) + adapter_scale * adapter_update).astype(
        jnp.bfloat16
    )
    projected_rows = lax.all_to_all(
        projected_sequence, "ctx", split_axis=2, concat_axis=1, tiled=True
    )
    seq_total = projected_rows.shape[1]
    head_view = projected_rows.reshape(3, seq_total, local_heads, HEAD_DIM)
    grad_view = grad_heads.reshape(seq_total, local_heads, HEAD_DIM)
    attended, query_grad, key_grad, value_grad = attend_heads(
        head_view[0], head_view[1], head_view[2], grad_view, local_flags
    )
    context = lax.all_to_all(
        attended.reshape(seq_total, local_width), "ctx", split_axis=0, concat_axis=1, tiled=True
    )
    grad_stack = jnp.stack([query_grad, key_grad, value_grad]).reshape(3, seq_total, local_width)
    token_gradient = lax.all_to_all(grad_stack, "ctx", split_axis=1, concat_axis=2, tiled=True)
    up_contribution = adapter_scale * jnp.einsum(
        "xvq,xvh->xqh", reduced_rank_rows, token_gradient, preferred_element_type=jnp.float32
    )
    backward_rank_rows = jnp.einsum(
        "efu,eau->efa", token_gradient, adapter_up_maps, preferred_element_type=jnp.float32
    ).astype(jnp.bfloat16)
    down_contribution = adapter_scale * jnp.einsum(
        "ow,noi->nwi", hidden_rows, backward_rank_rows, preferred_element_type=jnp.float32
    )
    grad_down, grad_up = lax.psum((down_contribution, up_contribution), ("dp", "ctx"))
    return (context[None], grad_down, grad_up)


def solution(mesh):
    placed = (
        P("dp", "ctx", None),
        P("dp", "ctx", None),
        P("dp", "ctx", None),
        P("dp", "ctx", None),
        P("dp", "ctx", None),
        P(),
        P(),
        P(),
    )
    return jax.shard_map(
        body,
        mesh=mesh,
        in_specs=placed,
        out_specs=(P("dp", "ctx", None), P(), P()),
        check_vma=False,
    )
```

profile of v0, /device:TPU:1, one launch (start us, length us, event | category | flops | bytes accessed | tf_op | source)
XLA Modules:
  0.0 670.3 jit_solution(5635035876560614335)
XLA Ops:
  7.2 2.4 copy.90
  9.6 11.8 %all-to-all-start.1 = ((bf16[128,32,128]{0,2,1:T(8,128)(2,1)}), bf16[128,32,128]{0,2,1:T(8,128)(2,1)S(1)}, u32[]{:S(2)}, u32[]{:S(2)}) async-start(bf16[128,32,128]{0,2,1:T(8,128)(2,1)} %bitcast.39), calls=%async_computation.1 | async-start | bytes 2097152 | tf_op jit(solution)/shard_map/all_to_all | solution.py:98
  22.6 3.8 add_convert_fusion
  26.3 7.1 %copy.79 = bf16[3,128,4096]{1,0,2:T(4,128)(2,1)} copy(bf16[3,128,4096]{2,1,0:T(8,128)(2,1)} %add_convert_fusion) | data formatting | bytes 6291456 | tf_op jit(solution)/shard_map/convert_element_type | solution.py:105
  33.4 14.2 %all-to-all-done.1 = bf16[128,32,128]{0,2,1:T(8,128)(2,1)S(1)} async-done(((bf16[128,32,128]{0,2,1:T(8,128)(2,1)}), bf16[128,32,128]{0,2,1:T(8,128)(2,1)S(1)}, u32[]{:S(2)}, u32[]{:S(2)}) %all-to-all-start.1) | async-done | bytes 1048608 | tf_op jit(solution)/shard_map/all_to_all | solution.py:98
  47.6 6.7 all-to-all-start
  57.4 1.6 copy.91
  59.2 1.2 broadcast_select_fusion
  60.4 86.4 %all-to-all-done = bf16[3,128,4096]{1,0,2:T(4,128)(2,1)} async-done(((bf16[3,128,4096]{1,0,2:T(4,128)(2,1)}), bf16[3,128,4096]{1,0,2:T(4,128)(2,1)}, u32[]{:S(2)}, u32[]{:S(2)}) %all-to-all-start) | async-done | bytes 3145760 | tf_op jit(solution)/shard_map/all_to_all | solution.py:108
  146.8 2.6 copy.80
  149.5 1.6 fusion.47
  151.7 1.7 fusion.46
  153.4 1.3 copy.87
  155.5 2.2 copy.84
  157.8 1.6 copy.86
  159.4 2.3 copy.81
  162.7 2.3 copy.83
  165.0 1.3 pad_maximum_fusion.2
  166.3 1.1 select_bitcast_fusion
  170.1 81.5 %while.16 = (s32[]{:T(128)}, bf16[4,1024,1,128]{3,1,0,2:T(8,128)(2,1)}, bf16[4,1024,1,128]{3,1,0,2:T(8,128)(2,1)}, bf16[4,1024,1,128]{3,1,0,2:T(8,128)(2,1)}, bf...) while((s32[]{:T(128)}, ...), condition=%wide.region_4.5_spmd, body=%wide.region_0.4_spmd.sunk | while | flops 1642329088 | bytes 69517472 | solution.py:66
  170.1 1.7 fusion.78
  172.4 1.2 constant_dynamic-slice_fusion.2
  175.7 3.9 fusion.80
  179.6 1.9 multiply_convert_fusion.2
  181.5 2.5 fusion.83
  185.1 1.8 constant_dynamic-update-slice_fusion.7
  186.9 1.4 fusion.81
  190.4 1.7 fusion.78
  192.7 1.2 constant_dynamic-slice_fusion.2
  196.1 3.9 fusion.80
  199.9 1.9 multiply_convert_fusion.2
  201.8 2.5 fusion.83
  205.4 1.8 constant_dynamic-update-slice_fusion.7
  207.2 1.4 fusion.81
  208.8 1.1 copy.141
  210.8 1.7 fusion.78
  213.1 1.2 constant_dynamic-slice_fusion.2
  216.4 3.9 fusion.80
  220.3 1.9 multiply_convert_fusion.2
  222.2 2.5 fusion.83
  225.8 1.8 constant_dynamic-update-slice_fusion.7
  227.6 1.4 fusion.81
  231.2 1.7 fusion.78
  233.4 1.2 constant_dynamic-slice_fusion.2
  236.8 3.9 fusion.80
  240.7 1.9 multiply_convert_fusion.2
  242.6 2.5 fusion.83
  246.2 1.8 constant_dynamic-update-slice_fusion.7
  248.0 1.4 fusion.81
  251.5 1.3 slice_bitcast_fusion.1
  253.9 1.2 slice_bitcast_fusion.2
  257.6 20.8 %copy.107 = bf16[3,4096,128]{2,0,1:T(4,128)(2,1)} copy(bf16[3,4096,128]{2,1,0:T(8,128)(2,1)S(1)} %maximum_bitcast_fusion) | data formatting | bytes 6291456 | tf_op jit(solution)/shard_map/reshape | solution.py:120
  278.4 7.4 %all-to-all-start.3 = ((bf16[3,4096,128]{2,0,1:T(4,128)(2,1)}), bf16[3,4096,128]{2,0,1:T(4,128)(2,1)}, u32[]{:S(2)}, u32[]{:S(2)}) async-start(bf16[3,4096,128]{2,0,1:T(4,128)(2,1)} %copy.107), calls=%async_computation.3 | async-start | bytes 8388608 | tf_op jit(solution)/shard_map/all_to_all | solution.py:121
  287.1 91.5 %all-to-all-done.3 = bf16[3,4096,128]{2,0,1:T(4,128)(2,1)} async-done(((bf16[3,4096,128]{2,0,1:T(4,128)(2,1)}), bf16[3,4096,128]{2,0,1:T(4,128)(2,1)}, u32[]{:S(2)}, u32[]{:S(2)}) %all-to-all-start.3) | async-done | bytes 3145760 | tf_op jit(solution)/shard_map/all_to_all | solution.py:121
  378.5 6.6 all-to-all-start.2
  385.2 2.7 copy.108
  387.9 1.6 copy-done.3
  389.5 1.4 convolution_multiply_fusion.2
  390.9 4.2 fusion.33
  395.2 14.8 %all-to-all-done.2 = bf16[32,128,128]{2,1,0:T(8,128)(2,1)S(1)} async-done(((bf16[32,128,128]{2,1,0:T(8,128)(2,1)}), bf16[32,128,128]{2,1,0:T(8,128)(2,1)S(1)}, u32[]{:S(2)}, u32[]{:S(2)}) %all-to-all-start.2) | async-done | bytes 1048608 | tf_op jit(solution)/shard_map/all_to_all | solution.py:117
  410.6 1.3 copy.110
  411.9 247.4 %all-reduce.3.cloned.1.call-done = (f32[3,4096,16]{1,2,0:T(8,128)}, f32[3,16,4096]{2,1,0:T(8,128)}) async-done(((f32[3,4096,16]{1,2,0:T(8,128)}, f32[3,16,4096]{2,1,0:T(8,128)}), (f32[3,4096,16]{1,2,0:T(8,128)}, f32[3,16,4096]{2,1,0:T(8,128)})) %all-reduce.3.cloned.1.call-update) | async-done | bytes 1572880 | tf_op jit(solution)/shard_map/psum | solution.py:131
  659.3 2.1 copy.167
  661.4 2.1 copy.168
  (110 shorter events, 36.8 us)
Async XLA Ops:
  7.2 14.3 %copy-start = (bf16[1,128,4096]{2,1,0:T(8,128)(2,1)S(1)}, bf16[1,128,4096]{2,1,0:T(8,128)(2,1)}, u32[]{:S(2)}) copy-start(bf16[1,128,4096]{2,1,0:T(8,128)(2,1)} %param.10) | copy-start | bytes 3145732
  7.2 14.3 %copy-start.11 = (bf16[3,4096,16]{1,2,0:T(8,128)(2,1)S(1)}, bf16[3,4096,16]{1,2,0:T(8,128)(2,1)}, u32[]{:S(2)}) copy-start(bf16[3,4096,16]{1,2,0:T(8,128)(2,1)} %param.15) | copy-start | bytes 1179652
  7.2 15.4 %copy-start.12 = (bf16[3,16,4096]{2,1,0:T(8,128)(2,1)S(1)}, bf16[3,16,4096]{2,1,0:T(8,128)(2,1)}, u32[]{:S(2)}) copy-start(bf16[3,16,4096]{2,1,0:T(8,128)(2,1)} %param.16) | copy-start | bytes 1179652
  9.6 38.1 %all-to-all-start.1 = ((bf16[128,32,128]{0,2,1:T(8,128)(2,1)}), bf16[128,32,128]{0,2,1:T(8,128)(2,1)S(1)}, u32[]{:S(2)}, u32[]{:S(2)}) async-start(bf16[128,32,128]{0,2,1:T(8,128)(2,1)} %bitcast.39), calls=%async_computation.1 | async-start | bytes 2097152 | tf_op jit(solution)/shard_map/all_to_all | solution.py:98
  22.0 0.6 copy-start.14
  33.4 21.0 %copy-start.16 = (s32[32]{0:T(128)S(1)}, s32[32]{0:T(128)}, u32[]{:S(2)}) copy-start(s32[32]{0:T(128)} %param.17) | copy-start | bytes 388
  47.6 99.2 %all-to-all-start = ((bf16[3,128,4096]{1,0,2:T(4,128)(2,1)}), bf16[3,128,4096]{1,0,2:T(4,128)(2,1)}, u32[]{:S(2)}, u32[]{:S(2)}) async-start(bf16[3,128,4096]{1,0,2:T(4,128)(2,1)} %copy.79), calls=%async_computation | async-start | bytes 8388608 | tf_op jit(solution)/shard_map/all_to_all | solution.py:108
  165.0 2.5 copy-start.9
  166.3 2.3 copy-start.10
  167.5 1.5 copy-start.8
  171.8 2.0 copy-start.1
  175.7 3.9 copy-start.2
  192.2 2.0 copy-start.1
  196.0 3.9 copy-start.2
  212.5 2.0 copy-start.1
  216.4 3.9 copy-start.2
  232.9 2.0 copy-start.1
  236.8 3.9 copy-start.2
  251.5 4.6 copy-start.7
  252.9 3.7 copy-start.4
  252.9 3.7 copy-start.5
  278.4 7.4 %copy-start.6 = (bf16[4,1024,1,128]{3,1,0,2:T(8,128)(2,1)S(1)}, bf16[4,1024,1,128]{3,1,0,2:T(8,128)(2,1)}, u32[]{:S(2)}) copy-start(bf16[4,1024,1,128]{3,1,0,2:T(8,128)(2,1)} %get-tuple-element.53) | copy-start | bytes 3145732
  278.4 100.1 %all-to-all-start.3 = ((bf16[3,4096,128]{2,0,1:T(4,128)(2,1)}), bf16[3,4096,128]{2,0,1:T(4,128)(2,1)}, u32[]{:S(2)}, u32[]{:S(2)}) async-start(bf16[3,4096,128]{2,0,1:T(4,128)(2,1)} %copy.107), calls=%async_computation.3 | async-start | bytes 8388608 | tf_op jit(solution)/shard_map/all_to_all | solution.py:121
  378.5 31.4 %all-to-all-start.2 = ((bf16[32,128,128]{2,1,0:T(8,128)(2,1)}), bf16[32,128,128]{2,1,0:T(8,128)(2,1)S(1)}, u32[]{:S(2)}, u32[]{:S(2)}) async-start(bf16[32,128,128]{2,1,0:T(8,128)(2,1)} %broadcast_select_fusion.1), calls=%async_computation.2 | async-start | bytes 2097152 | tf_op jit(solution)/shard_map/all_to_all | solution.py:117
  385.1 4.4 copy-start.15
  385.1 5.8 copy-start.13
  385.2 274.2 %all-reduce.3.cloned.1.call-start = ((), (), s32[]{:S(2)}) async-start(), calls=%async_computation.4 | async-start | bytes 3145728 | tf_op jit(solution)/shard_map/psum | solution.py:131
  387.9 1.6 copy-start.3
Sparse Core Ops, SparseCore 0:
  395.3 263.9 all-reduce.2
where the time goes:
time: 673 us; the launch traced here: 670 us
  waiting for transfers between devices  454 us (67%)
  local copies, waits for them, and re-layouts  98.2 us (15%)
  matrix products  59.2 us (9%)
  starting transfers between devices  32.6 us (5%)
  between operations  15.1 us (2%)
  other arithmetic  10.7 us (2%)
    psum x1, waiting for transfers between devices, body(): lax.psum((down_contribution, up_contribution), ('dp', 'ctx'))  247 us
    all_to_all x1, waiting for transfers between devices, body(): lax.all_to_all(grad_stack, 'ctx', split_axis=1, concat_axis=2, tiled=True)  91.5 us
    all_to_all x1, waiting for transfers between devices, body(): lax.all_to_all(projected_sequence, 'ctx', split_axis=2, concat_axis=1, ti...  86.4 us
    dynamic_update_slice x24, local copies, waits for them, and re-layouts, attend_heads(): lax.map(group_block, (regroup(queries), regroup(key_rows), regroup(value_...  23.5 us
    reshape x1, local copies, waits for them, and re-layouts, body(): jnp.stack([query_grad, key_grad, value_grad])  20.8 us
    dot_general x4, matrix products, group_block(): jnp.einsum('hqk,khe->qhe', weights_low, value_rows, preferred_element_typ...  15.5 us
    all_to_all x1, waiting for transfers between devices, body(): lax.all_to_all(attended.reshape(seq_total, local_width), 'ctx', split_axi...  14.8 us
    all_to_all x1, waiting for transfers between devices, body(): lax.all_to_all(cotangent[0], 'ctx', split_axis=1, concat_axis=0, tiled=True)  14.2 us
  transfers between devices with their start and end apart: 5, of which 5 were waited for; matrix products, arithmetic and copies ran while one was open for 4% of the time, Pallas kernels for 0%

commit v1 on v0

v1 whole, which is shorter than its diff:
```python
import functools
import math

import jax
import jax.numpy as jnp
from jax import lax
from jax.experimental import pallas as pl
from jax.experimental.pallas import tpu as pltpu
from jax.sharding import PartitionSpec as P

MESH = pl.DeviceIdType.MESH
HEAD_DIM = 128
RANK = 16
MAPS = 3
HEADS = 32
TOKENS = 128
MEMBERS = 8
CTX = 32
QUERY_BLOCK = 256
GROUP = MEMBERS * TOKENS
adapter_scale = 0.25
SOFTMAX_SCALE = 1.0 / math.sqrt(HEAD_DIM)
LOG2E = 1.4426950408889634
OFFSETS = (1, 3, 2, 4, 5, 7, 6)

BF = jnp.bfloat16
F32 = jnp.float32
NT = (((1,), (1,)), ((), ()))


def dot(a, b):
    return jnp.dot(a, b, preferred_element_type=F32)


def dot_nt(a, b):
    return lax.dot_general(a, b, NT, preferred_element_type=F32)


def place(me, kind):
    shifted = lax.rem(me + CTX - 4 * kind, CTX)
    position = lax.rem(shifted, MEMBERS)
    return position, shifted - position + 4 * kind


def partner(position, offset):
    half = lax.rem(position // 4 + offset // 4, 2)
    return half * 4 + lax.rem(lax.rem(position, 4) + offset % 4, 4)


def project_kernel(
    perm_ref, hidden_ref, query_ref, key_ref, value_ref, grad_ref, down_ref, up_ref, send_ref, low_ref, own_up_ref, low_rows
):
    step = pl.program_id(0)
    chunk, half = step // 2, lax.rem(step, 2)
    me = lax.axis_index("ctx")

    @pl.when(step == 0)
    def _():
        low_t = dot_nt(down_ref[...], hidden_ref[...])
        low_ref[...] = low_t.astype(BF)
        low_rows[...] = jnp.transpose(low_t).astype(BF)

    def columns_of(place_in_order):
        return pl.ds(pl.multiple_of(perm_ref[place_in_order] * HEAD_DIM, HEAD_DIM), HEAD_DIM)

    low = low_rows[...]
    first = 16 * (chunk // 2) + lax.rem(chunk, 2)
    for i in range(MEMBERS // 2):
        columns = columns_of(first + 2 * (half * (MEMBERS // 2) + i))
        for m, base_ref in enumerate((query_ref, key_ref, value_ref)):
            update = dot(low[:, m * RANK:(m + 1) * RANK], up_ref[m * RANK:(m + 1) * RANK, columns])
            send_ref[0, i, m * TOKENS:(m + 1) * TOKENS, :] = (
                base_ref[:, columns].astype(F32) + adapter_scale * update
            ).astype(BF)
        send_ref[0, i, 3 * TOKENS:4 * TOKENS, :] = grad_ref[:, columns]
    position, _ = place(me, chunk // 2)
    own_up_ref[chunk] = up_ref[:, columns_of(first + 2 * position)]


def restore_kernel(inv_ref, by_order_ref, context_ref):
    for head in range(HEADS):
        context_ref[:, head * HEAD_DIM:(head + 1) * HEAD_DIM] = by_order_ref[inv_ref[head]]


def attention_kernel(
    send_buf, low_own, own_up, hidden_ref,
    ctx_recv, grad_down_ref, grad_up_ref,
    recv_buf, low_buf, ctx_send, rank_send, rank_recv,
    kt_buf, vt_buf, gt_buf, dqt_buf, dk_buf, dv_buf,
    send_sem, recv_sem, low_send_sem, low_recv_sem, ctx_send_sem, ctx_recv_sem, rank_send_sem, rank_recv_sem,
):
    dp = lax.axis_index("dp")
    me = lax.axis_index("ctx")
    z, x = me // 4, lax.rem(me, 4)

    barrier = pltpu.get_barrier_semaphore()
    for dz in (-1, 0, 1):
        for dx in range(4):
            if dz == 0 and dx == 0:
                continue
            peer = lax.rem(z + dz + 8, 8) * 4 + lax.rem(x + dx, 4)
            pl.semaphore_signal(barrier, inc=1, device_id=(dp, peer), device_id_type=MESH)
    pl.semaphore_wait(barrier, 11)

    def low_copy(kind, offset):
        position, base = place(me, kind)
        target = partner(position, offset)
        return pltpu.make_async_remote_copy(
            src_ref=low_own, dst_ref=low_buf.at[kind, position],
            send_sem=low_send_sem.at[kind, offset], recv_sem=low_recv_sem.at[kind, offset],
            device_id=(dp, lax.rem(base + target, CTX)), device_id_type=MESH,
        )

    def data_copy(chunk, offset):
        position, base = place(me, chunk // 2)
        target = partner(position, offset)
        return pltpu.make_async_remote_copy(
            src_ref=send_buf.at[chunk, target], dst_ref=recv_buf.at[chunk, position],
            send_sem=send_sem.at[chunk, offset], recv_sem=recv_sem.at[chunk, offset],
            device_id=(dp, lax.rem(base + target, CTX)), device_id_type=MESH,
        )

    def context_copy(chunk, offset):
        kind = chunk // 2
        position, base = place(me, kind)
        target = partner(position, offset)
        return pltpu.make_async_remote_copy(
            src_ref=ctx_send.at[chunk, target],
            dst_ref=ctx_recv.at[16 * kind + 2 * position + lax.rem(chunk, 2)],
            send_sem=ctx_send_sem.at[chunk, offset], recv_sem=ctx_recv_sem.at[chunk, offset],
            device_id=(dp, lax.rem(base + target, CTX)), device_id_type=MESH,
        )

    def rank_copy(kind, offset):
        position, base = place(me, kind)
        target = partner(position, offset)
        return pltpu.make_async_remote_copy(
            src_ref=rank_send.at[kind, target], dst_ref=rank_recv.at[kind, offset],
            send_sem=rank_send_sem.at[kind, offset], recv_sem=rank_recv_sem.at[kind, offset],
            device_id=(dp, lax.rem(base + target, CTX)), device_id_type=MESH,
        )

    def own_copy(chunk):
        position, _ = place(me, chunk // 2)
        return pltpu.make_async_copy(
            send_buf.at[chunk, position], recv_buf.at[chunk, position], recv_sem.at[chunk, 0]
        )

    def start(chunk, carry):
        for offset in OFFSETS:
            data_copy(chunk, offset).start()
        own_copy(chunk).start()
        return carry

    start(0, 0)
    for kind in range(2):
        position, _ = place(me, kind)
        low_buf[kind, position] = low_own[...]
        for offset in OFFSETS:
            low_copy(kind, offset).start()
    lax.fori_loop(1, 4, start, 0)
    rank_send[...] = jnp.zeros_like(rank_send)
    for kind in range(2):
        for offset in OFFSETS:
            low_copy(kind, offset).wait_recv()

    def attend(chunk, carry):
        kind = chunk // 2
        position, _ = place(me, kind)
        for offset in OFFSETS:
            data_copy(chunk, offset).wait_recv()
        own_copy(chunk).wait()

        def rows(array, first, count):
            part = recv_buf[chunk, first // TOKENS:(first + count) // TOKENS, array * TOKENS:(array + 1) * TOKENS, :]
            return part.reshape(count, HEAD_DIM)

        kt_buf[...] = jnp.transpose(rows(1, 0, GROUP))
        vt_buf[...] = jnp.transpose(rows(2, 0, GROUP))
        gt_buf[...] = jnp.transpose(rows(3, 0, GROUP))
        for block in reversed(range(GROUP // QUERY_BLOCK)):
            first = block * QUERY_BLOCK
            seen = first + QUERY_BLOCK
            queries = rows(0, first, QUERY_BLOCK)
            grads = rows(3, first, QUERY_BLOCK)
            keys = rows(1, 0, seen)
            values = rows(2, 0, seen)
            scores = dot_nt(keys, queries)
            key_ids = lax.broadcasted_iota(jnp.int32, (seen, QUERY_BLOCK), 0)
            query_ids = lax.broadcasted_iota(jnp.int32, (seen, QUERY_BLOCK), 1) + first
            scores = jnp.where(key_ids <= query_ids, scores, -1e30)
            highest = jnp.max(scores, axis=0, keepdims=True)
            exponent = jnp.exp2((scores - highest) * (SOFTMAX_SCALE * LOG2E))
            weights = exponent * (1.0 / jnp.sum(exponent, axis=0, keepdims=True))
            weights_low = weights.astype(BF)
            attended = dot(vt_buf[:, :seen], weights_low).astype(BF).astype(F32)
            weight_grad = dot_nt(values, grads)
            row_inner = jnp.sum(gt_buf[:, first:seen].astype(F32) * attended, axis=0, keepdims=True)
            score_low = (weights * (weight_grad - row_inner)).astype(BF)
            dqt_buf[:, first:seen] = (dot(kt_buf[:, :seen], score_low) * SOFTMAX_SCALE).astype(BF)
            dk = dot(score_low, queries)
            dv = dot(weights_low, grads)
            if seen == GROUP:
                dk_buf[...] = dk
                dv_buf[...] = dv
            else:
                dk_buf[:seen] += dk
                dv_buf[:seen] += dv
            out_rows = jnp.transpose(attended).astype(BF).reshape(QUERY_BLOCK // TOKENS, TOKENS, HEAD_DIM)
            ctx_send[chunk, first // TOKENS:seen // TOKENS] = out_rows
        for offset in OFFSETS:
            context_copy(chunk, offset).start()
        own = 16 * kind + 2 * position + lax.rem(chunk, 2)
        ctx_recv[own] = ctx_send[chunk, position]

        dqt = dqt_buf[...]
        dk = (dk_buf[...] * SOFTMAX_SCALE).astype(BF)
        dv = dv_buf[...].astype(BF)
        low_all = jnp.concatenate([low_buf[kind, s] for s in range(MEMBERS)], axis=1)
        up = own_up[chunk]
        grad_up_ref[chunk] = adapter_scale * jnp.concatenate(
            [dot_nt(low_all[0:16], dqt), dot(low_all[16:32], dk), dot(low_all[32:48], dv)], axis=0
        )
        ranks = jnp.concatenate([dot(up[0:16], dqt), dot_nt(up[16:32], dk), dot_nt(up[32:48], dv)], axis=0)
        for s in range(MEMBERS):
            rank_send[kind, s] += ranks[:, s * TOKENS:(s + 1) * TOKENS]

        @pl.when(lax.rem(chunk, 2) == 1)
        def _():
            for offset in OFFSETS:
                rank_copy(kind, offset).start()

        return carry

    lax.fori_loop(0, 4, attend, 0)

    for kind in range(2):
        for offset in OFFSETS:
            rank_copy(kind, offset).wait_recv()
    total = jnp.zeros((MAPS * RANK, TOKENS), F32)
    for kind in range(2):
        position, _ = place(me, kind)
        total += rank_send[kind, position]
        for offset in OFFSETS:
            total += rank_recv[kind, offset]
    grad_down_ref[...] = adapter_scale * dot(total.astype(BF), hidden_ref[...])

    def finish(chunk, carry):
        for offset in OFFSETS:
            context_copy(chunk, offset).wait_recv()
            context_copy(chunk, offset).wait_send()
            data_copy(chunk, offset).wait_send()
        return carry

    lax.fori_loop(0, 4, finish, 0)
    for kind in range(2):
        for offset in OFFSETS:
            low_copy(kind, offset).wait_send()
            rank_copy(kind, offset).wait_send()


def body(hidden, query, key, value, cotangent, down, up, mask):
    width = hidden.shape[2]
    order = jnp.arange(HEADS, dtype=jnp.int32)
    shifted = (mask == 1).astype(jnp.int32)
    ahead = (order[None, :] < order[:, None]).astype(jnp.int32)
    shifted_ahead = jnp.sum(ahead * shifted[None, :], axis=1)
    inverse = jnp.where(shifted == 1, HEADS // 2 + shifted_ahead, order - shifted_ahead)
    perm = jnp.sum(jnp.where(inverse[None, :] == order[:, None], order[None, :], 0), axis=1)

    vmem = pl.BlockSpec(memory_space=pltpu.VMEM)
    smem = pl.BlockSpec(memory_space=pltpu.SMEM)
    dma = pltpu.SemaphoreType.DMA
    any_space = pl.BlockSpec(memory_space=pl.ANY)
    whole = pl.BlockSpec((TOKENS, width), lambda i, p: (0, 0))
    maps = pl.BlockSpec((MAPS * RANK, width), lambda i, p: (0, 0))
    send, low_t, own_up = pl.pallas_call(
        project_kernel,
        grid_spec=pltpu.PrefetchScalarGridSpec(
            num_scalar_prefetch=1,
            grid=(8,),
            in_specs=[whole] * 5 + [maps] * 2,
            out_specs=(
                pl.BlockSpec((1, MEMBERS // 2, 4 * TOKENS, HEAD_DIM), lambda i, p: (i // 2, i % 2, 0, 0)),
                pl.BlockSpec((MAPS * RANK, TOKENS), lambda i, p: (0, 0)),
                pl.BlockSpec((4, MAPS * RANK, HEAD_DIM), lambda i, p: (0, 0, 0)),
            ),
            scratch_shapes=[pltpu.VMEM((TOKENS, MAPS * RANK), BF)],
        ),
        out_shape=(
            jax.ShapeDtypeStruct((4, MEMBERS, 4 * TOKENS, HEAD_DIM), BF),
            jax.ShapeDtypeStruct((MAPS * RANK, TOKENS), BF),
            jax.ShapeDtypeStruct((4, MAPS * RANK, HEAD_DIM), BF),
        ),
        compiler_params=pltpu.CompilerParams(vmem_limit_bytes=32 * 1024 * 1024),
        name="project",
    )(
        perm, hidden[0], query[0], key[0], value[0], cotangent[0],
        jnp.transpose(down, (0, 2, 1)).reshape(MAPS * RANK, width), up.reshape(MAPS * RANK, width),
    )
    by_order, grad_down, grad_up = pl.pallas_call(
        attention_kernel,
        out_shape=(
            jax.ShapeDtypeStruct((HEADS, TOKENS, HEAD_DIM), BF),
            jax.ShapeDtypeStruct((MAPS * RANK, width), F32),
            jax.ShapeDtypeStruct((4, MAPS * RANK, HEAD_DIM), F32),
        ),
        in_specs=[any_space, vmem, vmem, vmem],
        out_specs=(vmem, vmem, vmem),
        scratch_shapes=[
            pltpu.VMEM((4, MEMBERS, 4 * TOKENS, HEAD_DIM), BF),
            pltpu.VMEM((2, MEMBERS, MAPS * RANK, TOKENS), BF),
            pltpu.VMEM((4, MEMBERS, TOKENS, HEAD_DIM), BF),
            pltpu.VMEM((2, MEMBERS, MAPS * RANK, TOKENS), F32),
            pltpu.VMEM((2, MEMBERS, MAPS * RANK, TOKENS), F32),
            pltpu.VMEM((HEAD_DIM, GROUP), BF),
            pltpu.VMEM((HEAD_DIM, GROUP), BF),
            pltpu.VMEM((HEAD_DIM, GROUP), BF),
            pltpu.VMEM((HEAD_DIM, GROUP), BF),
            pltpu.VMEM((GROUP, HEAD_DIM), F32),
            pltpu.VMEM((GROUP, HEAD_DIM), F32),
            dma((4, MEMBERS)), dma((4, MEMBERS)), dma((2, MEMBERS)), dma((2, MEMBERS)),
            dma((4, MEMBERS)), dma((4, MEMBERS)), dma((2, MEMBERS)), dma((2, MEMBERS)),
        ],
        compiler_params=pltpu.CompilerParams(
            collective_id=0, has_side_effects=True, vmem_limit_bytes=40 * 1024 * 1024
        ),
        name="shifted_group_attention",
    )(send, low_t, own_up, hidden[0])
    context = pl.pallas_call(
        restore_kernel,
        out_shape=jax.ShapeDtypeStruct((TOKENS, width), BF),
        in_specs=[smem, vmem],
        out_specs=vmem,
        name="restore_heads",
    )(inverse, by_order)

    me = lax.axis_index("ctx")
    plain, _ = place(me, 0)
    moved, _ = place(me, 1)
    by_head = jnp.zeros((HEADS, MAPS * RANK, HEAD_DIM), F32)
    by_head = lax.dynamic_update_slice_in_dim(by_head, grad_up[0:2], 2 * plain, 0)
    by_head = lax.dynamic_update_slice_in_dim(by_head, grad_up[2:4], 16 + 2 * moved, 0)
    grad_down, by_head = lax.psum((grad_down, by_head), ("dp", "ctx"))
    grad_up = jnp.transpose(jnp.take(by_head, inverse, axis=0), (1, 0, 2)).reshape(MAPS, RANK, width)
    grad_down = jnp.transpose(grad_down.reshape(MAPS, RANK, width), (0, 2, 1))
    return context[None], grad_down, grad_up


def solution(mesh):
    placed = (P("dp", "ctx", None),) * 5 + (P(),) * 3
    return jax.shard_map(
        body, mesh=mesh, in_specs=placed, out_specs=(P("dp", "ctx", None), P(), P()), check_vma=False
    )
```

time: 673 us -> 371 us (0.55)
  waiting for transfers between devices: 454 us -> 257 us
  local copies, waits for them, and re-layouts: 98.2 us -> 14 us
  Pallas kernels: 0 us -> 82.6 us
  matrix products: 59.2 us -> 0 us
  starting transfers between devices: 32.6 us -> 0.04 us
  other arithmetic: 10.7 us -> 1.68 us
    all_to_all x4 -> x0, waiting for transfers between devices: 207 us -> none  [the longest x1 91.5 us: body(): lax.all_to_all(grad_stack, 'ctx', split_axis=1, concat_axis=2, tiled=True)]
    pallas_call x0 -> x3, Pallas kernels: none -> 82.6 us  [the longest x1 76.4 us: body(): pl.pallas_call(attention_kernel, out_shape=(jax.ShapeDtypeStruct((HEADS,...]
    dot_general x28 -> x0, matrix products: 59.2 us -> none  [the longest x4 15.5 us: group_block(): jnp.einsum('hqk,khe->qhe', weights_low, value_rows, preferred_element_typ...]
    all_to_all x4 -> x0, starting transfers between devices: 32.5 us -> none  [the longest x1 11.8 us: body(): lax.all_to_all(cotangent[0], 'ctx', split_axis=1, concat_axis=0, tiled=True)]
    dynamic_update_slice x24 -> x2, local copies, waits for them, and re-layouts: 23.5 us -> 0.02 us  [the longest x1 0.01 us: body(): lax.dynamic_update_slice_in_dim(by_head, grad_up[2:4], 16 + 2 * moved, 0)]
    reshape x1, local copies, waits for them, and re-layouts: 20.8 us -> 1.02 us  [body(): jnp.transpose(jnp.take(by_head, inverse, axis=0), (1, 0, 2))]
    slice x16 -> x0, local copies, waits for them, and re-layouts: 18.3 us -> none  [the longest x12 12.1 us: shift_heads(): rolled = jnp.roll(values, amount, axis=0)]
    psum x1, waiting for transfers between devices: 247 us -> 257 us  [body(): grad_down, by_head = lax.psum((grad_down, by_head), ('dp', 'ctx'))]
  transfers between devices with their start and end apart: 5 -> 1, of which waited for: 5 -> 1; matrix products, arithmetic and copies ran while one was open for 4% -> 0% of each run, Pallas kernels for 0% -> 1%
where the time goes in v1:
time: 371 us; the launch traced here: 370 us
  waiting for transfers between devices  257 us (69%)
  Pallas kernels  82.6 us (22%)
  between operations  14.2 us (4%)
  local copies, waits for them, and re-layouts  14 us (4%)
    psum x1, waiting for transfers between devices, body(): grad_down, by_head = lax.psum((grad_down, by_head), ('dp', 'ctx'))  257 us
    pallas_call x1, Pallas kernels, body(): pl.pallas_call(attention_kernel, out_shape=(jax.ShapeDtypeStruct((HEADS,...  76.4 us
    unnamed x27, local copies, waits for them, and re-layouts  10.8 us
  transfers between devices with their start and end apart: 1, of which 1 were waited for; matrix products, arithmetic and copies ran while one was open for 0% of the time, Pallas kernels for 1%

profile of v1, /device:TPU:1, one launch (start us, length us, event | category | flops | bytes accessed | tf_op | source)
XLA Modules:
  0.0 369.9 jit_solution(15902290338457930183)
XLA Ops:
  7.2 0.0 all-reduce.3.cloned.1.call-start
  7.2 0.7 compare_convert_fusion
  7.9 0.1 select_reduce_fusion.1
  8.0 0.7 compare_and_fusion
  8.7 0.0 copy-start.11
  8.7 0.1 select_reduce_fusion.perm_ref
  8.8 0.0 copy-start
  8.8 1.2 copy-done
  10.0 0.0 copy-start.3
  10.0 1.2 copy-done.3
  11.3 0.0 copy-start.4
  11.3 1.2 copy-done.4
  12.5 0.0 copy-start.5
  12.5 1.2 copy-done.5
  13.7 0.0 copy-start.6
  13.7 1.2 copy-done.6
  14.9 0.0 copy-start.7
  14.9 1.0 copy-done.7
  15.9 0.0 copy-start.8
  15.9 1.0 copy-done.8
  16.9 0.0 copy-start.1
  16.9 3.7 %project.1 = (bf16[4,8,512,128]{3,2,1,0:T(8,128)(2,1)S(1)}, bf16[48,128]{1,0:T(8,128)(2,1)S(1)}, bf16[4,48,128]{2,1,0:T(8,128)(2,1)S(1)}) custom-call(s32[32]{0:T(128)S(1)} %select_reduce_fusion.perm_ref, bf16[128,4096]{1,0:T(8,128)(2,1)S(1)} %bitcast.15, bf16[128,4096]{1,0:T(8,128)(2,1)S(1)} %bitcast.17, bf16[128,4096]{1,0:T(8,128)(2,1)S(1)} %bitcast.18, ...), custom_call_target="tpu_custom_call" | custom-call | tf_op jit(solution)/shard_map/project/pallas_call | solution.py:277
  20.7 0.0 copy-done.1
  20.7 76.4 %shifted_group_attention.1 = (bf16[32,128,128]{2,1,0:T(8,128)(2,1)S(1)}, f32[48,4096]{1,0:T(8,128)}, f32[4,48,128]{2,1,0:T(8,128)S(1)}) custom-call(bf16[4,8,512,128]{3,2,1,0:T(8,128)(2,1)S(1)} %get-tuple-element.9.send_buf, bf16[48,128]{1,0:T(8,128)(2,1)S(1)} %get-tuple-element.10.low_own, bf16[4,48,128]{2,1,0:T(8,128)(2,1)S(1)} %get-tuple-element.11.own_up, ...), custom_call_target="tpu_custom_call" | custom-call | tf_op jit(solution)/shard_map/shifted_group_attention/pallas_call | solution.py:301
  97.1 0.0 copy-done.11
  97.1 0.0 copy-start.2
  97.1 1.0 copy-done.2
  98.1 0.0 copy-start.12
  98.1 0.1 broadcast_in_dim.34
  98.2 0.0 copy-start.9
  98.2 0.9 copy-done.9
  99.1 0.0 all-reduce.3.cloned.1.call-update
  99.1 2.5 restore_heads.1
  101.6 0.0 copy-done.12
  101.6 257.3 %all-reduce.3.cloned.1.call-done = (f32[3,4096,16]{1,2,0:T(8,128)}, f32[32,48,128]{2,1,0:T(8,128)}) async-done(((f32[3,4096,16]{1,2,0:T(8,128)}, f32[32,48,128]{2,1,0:T(8,128)}), (f32[3,4096,16]{1,2,0:T(8,128)}, f32[32,48,128]{2,1,0:T(8,128)})) %all-reduce.3.cloned.1.call-update) | async-done | bytes 1572880 | tf_op jit(solution)/shard_map/psum | solution.py:344
  358.9 0.0 copy-start.10
  358.9 1.8 gather_fusion
  360.7 0.1 select_bitcast_fusion
  360.9 0.3 copy.12
  361.1 1.0 reshape.28
  362.1 0.0 copy-done.10
  362.2 0.9 copy.18
  (4 shorter events, 0.0 us)
Async XLA Ops:
  7.2 351.8 %all-reduce.3.cloned.1.call-start = ((), (), s32[]{:S(2)}) async-start(), calls=%async_computation | async-start | bytes 3145728 | tf_op jit(solution)/shard_map/psum | solution.py:344
  8.7 88.4 %copy-start.11 = (s32[32]{0:T(128)}, s32[32]{0:T(128)S(1)}, u32[]{:S(2)}) copy-start(s32[32]{0:T(128)S(1)} %get-tuple-element.18.inv_ref) | copy-start | bytes 388
  8.8 1.2 copy-start
  10.0 1.2 copy-start.3
  11.3 1.2 copy-start.4
  12.5 1.2 copy-start.5
  13.7 1.2 copy-start.6
  14.9 1.0 copy-start.7
  15.9 1.0 copy-start.8
  16.9 3.7 %copy-start.1 = (bf16[1,128,4096]{2,1,0:T(8,128)(2,1)S(1)}, bf16[1,128,4096]{2,1,0:T(8,128)(2,1)}, u32[]{:S(2)}) copy-start(bf16[1,128,4096]{2,1,0:T(8,128)(2,1)} %param.8) | copy-start | bytes 3145732
  97.1 1.0 copy-start.2
  98.1 3.5 copy-start.12
  98.2 0.9 copy-start.9
  358.9 3.2 copy-start.10
Sparse Core Ops, SparseCore 0:
  99.2 259.6 all-reduce.2

commit v2 on v1

--- a/solution.py
+++ b/solution.py
@@ -23,6 +23,12 @@
 LOG2E = 1.4426950408889634
 OFFSETS = (1, 3, 2, 4, 5, 7, 6)
 
+HALF = MAPS * RANK // 2
+PIECES = 16
+PIECE = 256
+PAIR_PARTS = 4
+PAIR_PIECES = PIECES // PAIR_PARTS
+
 BF = jnp.bfloat16
 F32 = jnp.float32
 NT = (((1,), (1,)), ((), ()))
@@ -77,9 +83,10 @@
     own_up_ref[chunk] = up_ref[:, columns_of(first + 2 * position)]
 
 
-def restore_kernel(inv_ref, by_order_ref, context_ref):
+def restore_kernel(inv_ref, by_order_ref, up_by_order_ref, context_ref, grad_up_ref):
     for head in range(HEADS):
         context_ref[:, head * HEAD_DIM:(head + 1) * HEAD_DIM] = by_order_ref[inv_ref[head]]
+        grad_up_ref[:, head * HEAD_DIM:(head + 1) * HEAD_DIM] = up_by_order_ref[inv_ref[head]]
 
 
 def attention_kernel(
@@ -87,11 +94,16 @@
     ctx_recv, grad_down_ref, grad_up_ref,
     recv_buf, low_buf, ctx_send, rank_send, rank_recv,
     kt_buf, vt_buf, gt_buf, dqt_buf, dk_buf, dv_buf,
+    down_part, down_pair, down_sum, down_recv, up_part, up_pair, up_sum, up_recv, line_buf, all_buf,
     send_sem, recv_sem, low_send_sem, low_recv_sem, ctx_send_sem, ctx_recv_sem, rank_send_sem, rank_recv_sem,
+    pair_send_sem, pair_recv_sem, plane_send_sem, plane_recv_sem, side_send_sem, side_recv_sem,
+    line_send_sem, line_recv_sem, all_send_sem, all_recv_sem, last_send_sem, last_recv_sem,
 ):
     dp = lax.axis_index("dp")
     me = lax.axis_index("ctx")
     z, x = me // 4, lax.rem(me, 4)
+    y, core = dp // 2, lax.rem(dp, 2)
+    own_piece = y * 4 + x
 
     barrier = pltpu.get_barrier_semaphore()
     for dz in (-1, 0, 1):
@@ -100,7 +112,15 @@
                 continue
             peer = lax.rem(z + dz + 8, 8) * 4 + lax.rem(x + dx, 4)
             pl.semaphore_signal(barrier, inc=1, device_id=(dp, peer), device_id_type=MESH)
-    pl.semaphore_wait(barrier, 11)
+    for dz in range(2, 7):
+        pl.semaphore_signal(barrier, inc=1, device_id=(dp, lax.rem(z + dz, 8) * 4 + x), device_id_type=MESH)
+    for dy in range(1, 4):
+        for dx in range(4):
+            peer = (lax.rem(y + dy, 4) * 2 + core, z * 4 + lax.rem(x + dx, 4))
+            pl.semaphore_signal(barrier, inc=1, device_id=peer, device_id_type=MESH)
+    sibling = (y * 2 + 1 - core, me)
+    pl.semaphore_signal(barrier, inc=1, device_id=sibling, device_id_type=MESH)
+    pl.semaphore_wait(barrier, 29)
 
     def low_copy(kind, offset):
         position, base = place(me, kind)
@@ -218,9 +238,11 @@
         dv = dv_buf[...].astype(BF)
         low_all = jnp.concatenate([low_buf[kind, s] for s in range(MEMBERS)], axis=1)
         up = own_up[chunk]
-        grad_up_ref[chunk] = adapter_scale * jnp.concatenate(
+        up_grad = adapter_scale * jnp.concatenate(
             [dot_nt(low_all[0:16], dqt), dot(low_all[16:32], dk), dot(low_all[32:48], dv)], axis=0
         )
+        up_part[0, chunk] = up_grad[:HALF]
+        up_part[1, chunk] = up_grad[HALF:]
         ranks = jnp.concatenate([dot(up[0:16], dqt), dot_nt(up[16:32], dk), dot_nt(up[32:48], dv)], axis=0)
         for s in range(MEMBERS):
             rank_send[kind, s] += ranks[:, s * TOKENS:(s + 1) * TOKENS]
@@ -243,7 +265,115 @@
         total += rank_send[kind, position]
         for offset in OFFSETS:
             total += rank_recv[kind, offset]
-    grad_down_ref[...] = adapter_scale * dot(total.astype(BF), hidden_ref[...])
+    total_low = total.astype(BF)
+
+    def pair_copy(part):
+        if part == PAIR_PARTS:
+            source, target = up_part.at[1 - core], up_pair
+        else:
+            span = pl.ds(part * PAIR_PIECES, PAIR_PIECES)
+            source, target = down_part.at[1 - core, span], down_pair.at[span]
+        return pltpu.make_async_remote_copy(
+            src_ref=source, dst_ref=target, send_sem=pair_send_sem.at[part], recv_sem=pair_recv_sem.at[part],
+            device_id=sibling, device_id_type=MESH,
+        )
+
+    def plane_device(offset):
+        to_y, to_x = lax.rem(y + offset // 4, 4), lax.rem(x + offset % 4, 4)
+        return to_y * 4 + to_x, (to_y * 2 + core, z * 4 + to_x)
+
+    def plane_copy(offset):
+        piece, device = plane_device(offset)
+        return pltpu.make_async_remote_copy(
+            src_ref=down_sum.at[piece], dst_ref=down_recv.at[offset],
+            send_sem=plane_send_sem.at[offset], recv_sem=plane_recv_sem.at[offset],
+            device_id=device, device_id_type=MESH,
+        )
+
+    def side_copy(offset):
+        to_y = lax.rem(y + offset, 4)
+        return pltpu.make_async_remote_copy(
+            src_ref=up_sum.at[to_y], dst_ref=up_recv.at[offset],
+            send_sem=side_send_sem.at[offset], recv_sem=side_recv_sem.at[offset],
+            device_id=(to_y * 2 + core, me), device_id_type=MESH,
+        )
+
+    def line_copy(offset):
+        return pltpu.make_async_remote_copy(
+            src_ref=line_buf.at[z], dst_ref=line_buf.at[z],
+            send_sem=line_send_sem.at[offset], recv_sem=line_recv_sem.at[offset],
+            device_id=(dp, lax.rem(z + offset, 8) * 4 + x), device_id_type=MESH,
+        )
+
+    def all_copy(offset):
+        _, device = plane_device(offset)
+        return pltpu.make_async_remote_copy(
+            src_ref=all_buf.at[core, own_piece], dst_ref=all_buf.at[core, own_piece],
+            send_sem=all_send_sem.at[offset], recv_sem=all_recv_sem.at[offset],
+            device_id=device, device_id_type=MESH,
+        )
+
+    def last_copy(offset):
+        piece = lax.rem(y + 4 - offset // 4, 4) * 4 + lax.rem(x + 4 - offset % 4, 4)
+        return pltpu.make_async_remote_copy(
+            src_ref=all_buf.at[core, piece], dst_ref=all_buf.at[core, piece],
+            send_sem=last_send_sem.at[offset], recv_sem=last_recv_sem.at[offset],
+            device_id=sibling, device_id_type=MESH,
+        )
+
+    pair_copy(PAIR_PARTS).start()
+    for part in range(PAIR_PARTS):
+        for piece in range(part * PAIR_PIECES, (part + 1) * PAIR_PIECES):
+            grads = adapter_scale * dot(total_low, hidden_ref[:, piece * PIECE:(piece + 1) * PIECE])
+            down_part[0, piece] = grads[:HALF]
+            down_part[1, piece] = grads[HALF:]
+        pair_copy(part).start()
+    pair_copy(PAIR_PARTS).wait_recv()
+    up_sum[...] = up_part[core] + up_pair[...]
+    for offset in range(1, 4):
+        side_copy(offset).start()
+    for part in range(PAIR_PARTS):
+        pair_copy(part).wait_recv()
+    down_sum[...] = down_part[core] + down_pair[...]
+    for offset in range(1, PIECES):
+        plane_copy(offset).start()
+
+    for offset in range(1, 4):
+        side_copy(offset).wait_recv()
+    line_buf[z, :, PIECE:] = ((up_sum[y] + up_recv[1]) + up_recv[2]) + up_recv[3]
+    reduced = down_sum[own_piece]
+    for offset in range(1, PIECES):
+        plane_copy(offset).wait_recv()
+        reduced = reduced + down_recv[offset]
+    line_buf[z, :, :PIECE] = reduced
+    for offset in range(1, 8):
+        line_copy(offset).start()
+    for offset in range(1, 8):
+        line_copy(offset).wait_recv()
+    even = line_buf[0] + line_buf[2] + (line_buf[4] + line_buf[6])
+    odd = line_buf[1] + line_buf[3] + (line_buf[5] + line_buf[7])
+    all_buf[core, own_piece, :, :PIECE] = even[:, :PIECE] + odd[:, :PIECE]
+    all_buf[core, own_piece, :, PIECE:PIECE + HEAD_DIM] = even[:, PIECE:]
+    all_buf[core, own_piece, :, PIECE + HEAD_DIM:] = odd[:, PIECE:]
+    for offset in range(1, PIECES):
+        all_copy(offset).start()
+    last_copy(0).start()
+    for offset in range(1, PIECES):
+        all_copy(offset).wait_recv()
+        last_copy(offset).start()
+    for offset in range(PIECES):
+        last_copy(offset).wait_recv()
+
+    for half in range(2):
+        for piece in range(PIECES):
+            at_y, at_x = piece // 4, piece % 4
+            rows_of = slice(half * HALF, (half + 1) * HALF)
+            grad_down_ref[rows_of, piece * PIECE:(piece + 1) * PIECE] = all_buf[half, piece, :, :PIECE]
+            for parity in range(2):
+                position = (parity if at_y < 2 else 1 - parity) * 4 + at_x
+                grad_up_ref[16 * (at_y // 2) + 2 * position + at_y % 2, rows_of] = all_buf[
+                    half, piece, :, PIECE + parity * HEAD_DIM:PIECE + (parity + 1) * HEAD_DIM
+                ]
 
     def finish(chunk, carry):
         for offset in OFFSETS:
@@ -257,6 +387,17 @@
         for offset in OFFSETS:
             low_copy(kind, offset).wait_send()
             rank_copy(kind, offset).wait_send()
+    for part in range(PAIR_PARTS + 1):
+        pair_copy(part).wait_send()
+    for offset in range(1, 4):
+        side_copy(offset).wait_send()
+    for offset in range(1, 8):
+        line_copy(offset).wait_send()
+    for offset in range(PIECES):
+        last_copy(offset).wait_send()
+        if offset:
+            plane_copy(offset).wait_send()
+            all_copy(offset).wait_send()
 
 
 def body(hidden, query, key, value, cotangent, down, up, mask):
@@ -303,7 +444,7 @@
         out_shape=(
             jax.ShapeDtypeStruct((HEADS, TOKENS, HEAD_DIM), BF),
             jax.ShapeDtypeStruct((MAPS * RANK, width), F32),
-            jax.ShapeDtypeStruct((4, MAPS * RANK, HEAD_DIM), F32),
+            jax.ShapeDtypeStruct((HEADS, MAPS * RANK, HEAD_DIM), F32),
         ),
         in_specs=[any_space, vmem, vmem, vmem],
         out_specs=(vmem, vmem, vmem),
@@ -319,30 +460,37 @@
             pltpu.VMEM((HEAD_DIM, GROUP), BF),
             pltpu.VMEM((GROUP, HEAD_DIM), F32),
             pltpu.VMEM((GROUP, HEAD_DIM), F32),
+            pltpu.VMEM((2, PIECES, HALF, PIECE), F32),
+            pltpu.VMEM((PIECES, HALF, PIECE), F32),
+            pltpu.VMEM((PIECES, HALF, PIECE), F32),
+            pltpu.VMEM((PIECES, HALF, PIECE), F32),
+            pltpu.VMEM((2, 4, HALF, HEAD_DIM), F32),
+            pltpu.VMEM((4, HALF, HEAD_DIM), F32),
+            pltpu.VMEM((4, HALF, HEAD_DIM), F32),
+            pltpu.VMEM((4, HALF, HEAD_DIM), F32),
+            pltpu.VMEM((8, HALF, PIECE + HEAD_DIM), F32),
+            pltpu.VMEM((2, PIECES, HALF, PIECE + 2 * HEAD_DIM), F32),
             dma((4, MEMBERS)), dma((4, MEMBERS)), dma((2, MEMBERS)), dma((2, MEMBERS)),
             dma((4, MEMBERS)), dma((4, MEMBERS)), dma((2, MEMBERS)), dma((2, MEMBERS)),
+            dma((PAIR_PARTS + 1,)), dma((PAIR_PARTS + 1,)), dma((PIECES,)), dma((PIECES,)), dma((4,)), dma((4,)),
+            dma((8,)), dma((8,)), dma((PIECES,)), dma((PIECES,)), dma((PIECES,)), dma((PIECES,)),
         ],
         compiler_params=pltpu.CompilerParams(
             collective_id=0, has_side_effects=True, vmem_limit_bytes=40 * 1024 * 1024
         ),
         name="shifted_group_attention",
     )(send, low_t, own_up, hidden[0])
-    context = pl.pallas_call(
+    context, grad_up = pl.pallas_call(
         restore_kernel,
-        out_shape=jax.ShapeDtypeStruct((TOKENS, width), BF),
-        in_specs=[smem, vmem],
-        out_specs=vmem,
+        out_shape=(
+            jax.ShapeDtypeStruct((TOKENS, width), BF),
+            jax.ShapeDtypeStruct((MAPS * RANK, width), F32),
+        ),
+        in_specs=[smem, vmem, vmem],
+        out_specs=(vmem, vmem),
         name="restore_heads",
-    )(inverse, by_order)
-
-    me = lax.axis_index("ctx")
-    plain, _ = place(me, 0)
-    moved, _ = place(me, 1)
-    by_head = jnp.zeros((HEADS, MAPS * RANK, HEAD_DIM), F32)
-    by_head = lax.dynamic_update_slice_in_dim(by_head, grad_up[0:2], 2 * plain, 0)
-    by_head = lax.dynamic_update_slice_in_dim(by_head, grad_up[2:4], 16 + 2 * moved, 0)
-    grad_down, by_head = lax.psum((grad_down, by_head), ("dp", "ctx"))
-    grad_up = jnp.transpose(jnp.take(by_head, inverse, axis=0), (1, 0, 2)).reshape(MAPS, RANK, width)
+    )(inverse, by_order, grad_up)
+    grad_up = grad_up.reshape(MAPS, RANK, width)
     grad_down = jnp.transpose(grad_down.reshape(MAPS, RANK, width), (0, 2, 1))
     return context[None], grad_down, grad_up
 

time: 371 us -> 133 us (0.36)
  waiting for transfers between devices: 257 us -> 0 us
  Pallas kernels: 82.6 us -> 119 us
  between operations: 14.2 us -> 0.69 us
    psum x1 -> x0, waiting for transfers between devices: 257 us -> none  [body(): grad_down, by_head = lax.psum((grad_down, by_head), ('dp', 'ctx'))]
    pallas_call x1, Pallas kernels: 76.4 us -> 113 us  [body(): pl.pallas_call(attention_kernel, out_shape=(jax.ShapeDtypeStruct((HEADS,...]
    unnamed x27 -> x23, local copies, waits for them, and re-layouts: 10.8 us -> 10.8 us
  transfers between devices with their start and end apart: 1 -> 0, of which waited for: 1 -> 0; matrix products, arithmetic and copies ran while one was open for 0% -> 0% of each run, Pallas kernels for 1% -> 0%
where the time goes in v2:
time: 133 us
  Pallas kernels  119 us (89%)
  local copies, waits for them, and re-layouts  10.8 us (8%)
  other arithmetic  1.55 us (1%)
    pallas_call x1, Pallas kernels, body(): pl.pallas_call(attention_kernel, out_shape=(jax.ShapeDtypeStruct((HEADS,...  113 us
    unnamed x23, local copies, waits for them, and re-layouts  10.8 us
    pallas_call x1, Pallas kernels, body(): pl.pallas_call(project_kernel, grid_spec=pltpu.PrefetchScalarGridSpec(num...  3.71 us
    pallas_call x1, Pallas kernels, body(): pl.pallas_call(restore_kernel, out_shape=(jax.ShapeDtypeStruct((TOKENS, w...  3.03 us

profile of v2, /device:TPU:1, one launch (start us, length us, event | category | flops | bytes accessed | tf_op | source)
XLA Modules:
  0.0 132.6 jit_solution(13758371806731153071)
XLA Ops:
  0.6 0.7 compare_convert_fusion
  1.3 0.1 select_reduce_fusion.1
  1.4 0.7 compare_select_fusion.inv_ref
  2.1 0.0 copy-start.10
  2.1 0.1 select_reduce_fusion.perm_ref
  2.2 0.0 copy-start
  2.2 1.2 copy-done
  3.4 0.0 copy-start.3
  3.4 1.2 copy-done.3
  4.6 0.0 copy-start.4
  4.6 1.2 copy-done.4
  5.9 0.0 copy-start.5
  5.9 1.2 copy-done.5
  7.1 0.0 copy-start.6
  7.1 1.2 copy-done.6
  8.3 0.0 copy-start.8
  8.3 1.0 copy-done.8
  9.3 0.0 copy-start.9
  9.3 1.0 copy-done.9
  10.3 0.0 copy-start.1
  10.3 3.7 %project.1 = (bf16[4,8,512,128]{3,2,1,0:T(8,128)(2,1)S(1)}, bf16[48,128]{1,0:T(8,128)(2,1)S(1)}, bf16[4,48,128]{2,1,0:T(8,128)(2,1)S(1)}) custom-call(s32[32]{0:T(128)S(1)} %select_reduce_fusion.perm_ref, bf16[128,4096]{1,0:T(8,128)(2,1)S(1)} %bitcast.14, bf16[128,4096]{1,0:T(8,128)(2,1)S(1)} %bitcast.16, bf16[128,4096]{1,0:T(8,128)(2,1)S(1)} %bitcast.17, ...), custom_call_target="tpu_custom_call" | custom-call | tf_op jit(solution)/shard_map/project/pallas_call | solution.py:418
  14.0 0.0 copy-done.1
  14.0 112.7 %shifted_group_attention.1 = (bf16[32,128,128]{2,1,0:T(8,128)(2,1)S(1)}, f32[48,4096]{1,0:T(8,128)S(1)}, f32[32,48,128]{2,1,0:T(8,128)S(1)}) custom-call(bf16[4,8,512,128]{3,2,1,0:T(8,128)(2,1)S(1)} %get-tuple-element.11.send_buf, bf16[48,128]{1,0:T(8,128)(2,1)S(1)} %get-tuple-element.12.low_own, bf16[4,48,128]{2,1,0:T(8,128)(2,1)S(1)} %get-tuple-element.13.own_up, ...), custom_call_target="tpu_custom_call" | custom-call | tf_op jit(solution)/shard_map/shifted_group_attention/pallas_call | solution.py:442
  126.8 0.0 copy-done.10
  126.8 0.0 copy-start.2
  126.8 1.0 copy-done.2
  127.8 0.0 copy-start.7
  127.8 0.9 copy-done.7
  128.6 3.0 %restore_heads.1 = (bf16[128,4096]{1,0:T(8,128)(2,1)}, f32[48,4096]{1,0:T(8,128)}) custom-call(s32[32]{0:T(128)} %copy-done.10, bf16[32,128,128]{2,1,0:T(8,128)(2,1)} %copy-done.2, f32[32,48,128]{2,1,0:T(8,128)} %copy-done.7), custom_call_target="tpu_custom_call" | custom-call | tf_op jit(solution)/shard_map/restore_heads/pallas_call | solution.py:483
  131.7 0.9 copy.12
Async XLA Ops:
  2.1 124.7 %copy-start.10 = (s32[32]{0:T(128)}, s32[32]{0:T(128)S(1)}, u32[]{:S(2)}) copy-start(s32[32]{0:T(128)S(1)} %compare_select_fusion.inv_ref) | copy-start | bytes 388
  2.2 1.2 copy-start
  3.4 1.2 copy-start.3
  4.6 1.2 copy-start.4
  5.9 1.2 copy-start.5
  7.1 1.2 copy-start.6
  8.3 1.0 copy-start.8
  9.3 1.0 copy-start.9
  10.3 3.7 %copy-start.1 = (bf16[1,128,4096]{2,1,0:T(8,128)(2,1)S(1)}, bf16[1,128,4096]{2,1,0:T(8,128)(2,1)}, u32[]{:S(2)}) copy-start(bf16[1,128,4096]{2,1,0:T(8,128)(2,1)} %param.8) | copy-start | bytes 3145732
  126.8 1.0 copy-start.2
  127.8 0.9 copy-start.7

commit v3 on v2

--- a/solution.py
+++ b/solution.py
@@ -25,7 +25,9 @@
 
 HALF = MAPS * RANK // 2
 PIECES = 16
-PIECE = 256
+PIECE = 128
+DEFER = True
+VMEM_GRANT = 62 * 1024 * 1024
 PAIR_PARTS = 4
 PAIR_PIECES = PIECES // PAIR_PARTS
 
@@ -53,8 +55,18 @@
     return half * 4 + lax.rem(lax.rem(position, 4) + offset % 4, 4)
 
 
+def head_positions(mask_ref, visit):
+    def step(head, shifted_before):
+        flag = mask_ref[head]
+        visit(head, jnp.where(flag == 1, HEADS // 2 + shifted_before, head - shifted_before))
+        return shifted_before + flag
+
+    lax.fori_loop(0, HEADS, step, jnp.int32(0))
+
+
 def project_kernel(
-    perm_ref, hidden_ref, query_ref, key_ref, value_ref, grad_ref, down_ref, up_ref, send_ref, low_ref, own_up_ref, low_rows
+    mask_ref, hidden_ref, query_ref, key_ref, value_ref, grad_ref, down_ref, up_ref,
+    send_ref, low_ref, own_up_ref, low_rows, perm_ref,
 ):
     step = pl.program_id(0)
     chunk, half = step // 2, lax.rem(step, 2)
@@ -62,6 +74,10 @@
 
     @pl.when(step == 0)
     def _():
+        def visit(head, position):
+            perm_ref[position] = head
+
+        head_positions(mask_ref, visit)
         low_t = dot_nt(down_ref[...], hidden_ref[...])
         low_ref[...] = low_t.astype(BF)
         low_rows[...] = jnp.transpose(low_t).astype(BF)
@@ -83,21 +99,39 @@
     own_up_ref[chunk] = up_ref[:, columns_of(first + 2 * position)]
 
 
-def restore_kernel(inv_ref, by_order_ref, up_by_order_ref, context_ref, grad_up_ref):
+def restore_kernel(mask_ref, by_order_ref, all_ref, context_ref, grad_down_ref, grad_up_ref, sems):
+    def copy(head, position):
+        columns = pl.ds(pl.multiple_of(head * HEAD_DIM, HEAD_DIM), HEAD_DIM)
+        return pltpu.make_async_copy(by_order_ref.at[position], context_ref.at[:, columns], sems.at[head])
+
+    head_positions(mask_ref, lambda head, position: copy(head, position).start())
+    for core in range(2):
+        for piece in range(PIECES):
+            first = core * PIECES * PIECE + piece * PIECE
+            grad_down_ref[:, first:first + PIECE] = all_ref[core, piece, 0].astype(F32)
+
+    def restore(head, position):
+        kind, member = position // 16, lax.rem(position, 16) // 2
+        parity = jnp.where(kind == 0, member // 4, 1 - member // 4)
+        columns = pl.ds(pl.multiple_of(head * HEAD_DIM, HEAD_DIM), HEAD_DIM)
+        for part in range(2):
+            pieces = all_ref[kind, (2 * lax.rem(position, 2) + part) * 4 + lax.rem(member, 4), 1].astype(F32)
+            grad_up_ref[part * HALF:(part + 1) * HALF, columns] = jnp.where(parity == 0, pieces[:HALF], pieces[HALF:])
+
+    head_positions(mask_ref, restore)
     for head in range(HEADS):
-        context_ref[:, head * HEAD_DIM:(head + 1) * HEAD_DIM] = by_order_ref[inv_ref[head]]
-        grad_up_ref[:, head * HEAD_DIM:(head + 1) * HEAD_DIM] = up_by_order_ref[inv_ref[head]]
+        copy(head, 0).wait()
 
 
 def attention_kernel(
     send_buf, low_own, own_up, hidden_ref,
-    ctx_recv, grad_down_ref, grad_up_ref,
+    ctx_recv, all_buf,
     recv_buf, low_buf, ctx_send, rank_send, rank_recv,
     kt_buf, vt_buf, gt_buf, dqt_buf, dk_buf, dv_buf,
-    down_part, down_pair, down_sum, down_recv, up_part, up_pair, up_sum, up_recv, line_buf, all_buf,
+    down_part, down_pair, down_sum, down_recv, up_part, up_pair, up_sum, up_recv, line_buf, up_line_buf,
     send_sem, recv_sem, low_send_sem, low_recv_sem, ctx_send_sem, ctx_recv_sem, rank_send_sem, rank_recv_sem,
     pair_send_sem, pair_recv_sem, plane_send_sem, plane_recv_sem, side_send_sem, side_recv_sem,
-    line_send_sem, line_recv_sem, all_send_sem, all_recv_sem, last_send_sem, last_recv_sem,
+    line_send_sem, line_recv_sem, up_line_send_sem, up_line_recv_sem, own_sem, all_send_sem, all_recv_sem, last_send_sem, last_recv_sem,
 ):
     dp = lax.axis_index("dp")
     me = lax.axis_index("ctx")
@@ -184,12 +218,27 @@
         for offset in OFFSETS:
             low_copy(kind, offset).wait_recv()
 
+    def own_context(chunk):
+        kind = chunk // 2
+        position, _ = place(me, kind)
+        return pltpu.make_async_copy(
+            ctx_send.at[chunk, position], ctx_recv.at[16 * kind + 2 * position + lax.rem(chunk, 2)], own_sem.at[chunk]
+        )
+
+    def send_context(chunk):
+        for offset in OFFSETS:
+            context_copy(chunk, offset).start()
+        own_context(chunk).start()
+
     def attend(chunk, carry):
         kind = chunk // 2
-        position, _ = place(me, kind)
         for offset in OFFSETS:
             data_copy(chunk, offset).wait_recv()
         own_copy(chunk).wait()
+        if DEFER:
+            @pl.when(chunk == 3)
+            def _():
+                lax.fori_loop(0, 3, lambda c, carry: (send_context(c), carry)[1], 0)
 
         def rows(array, first, count):
             part = recv_buf[chunk, first // TOKENS:(first + count) // TOKENS, array * TOKENS:(array + 1) * TOKENS, :]
@@ -228,10 +277,8 @@
                 dv_buf[:seen] += dv
             out_rows = jnp.transpose(attended).astype(BF).reshape(QUERY_BLOCK // TOKENS, TOKENS, HEAD_DIM)
             ctx_send[chunk, first // TOKENS:seen // TOKENS] = out_rows
-        for offset in OFFSETS:
-            context_copy(chunk, offset).start()
-        own = 16 * kind + 2 * position + lax.rem(chunk, 2)
-        ctx_recv[own] = ctx_send[chunk, position]
+        if not DEFER:
+            send_context(chunk)
 
         dqt = dqt_buf[...]
         dk = (dk_buf[...] * SOFTMAX_SCALE).astype(BF)
@@ -241,8 +288,8 @@
         up_grad = adapter_scale * jnp.concatenate(
             [dot_nt(low_all[0:16], dqt), dot(low_all[16:32], dk), dot(low_all[32:48], dv)], axis=0
         )
-        up_part[0, chunk] = up_grad[:HALF]
-        up_part[1, chunk] = up_grad[HALF:]
+        up_part[kind, 2 * lax.rem(chunk, 2)] = up_grad[:HALF]
+        up_part[kind, 2 * lax.rem(chunk, 2) + 1] = up_grad[HALF:]
         ranks = jnp.concatenate([dot(up[0:16], dqt), dot_nt(up[16:32], dk), dot_nt(up[32:48], dv)], axis=0)
         for s in range(MEMBERS):
             rank_send[kind, s] += ranks[:, s * TOKENS:(s + 1) * TOKENS]
@@ -305,6 +352,13 @@
             device_id=(dp, lax.rem(z + offset, 8) * 4 + x), device_id_type=MESH,
         )
 
+    def up_line_copy(offset):
+        return pltpu.make_async_remote_copy(
+            src_ref=up_line_buf.at[z], dst_ref=up_line_buf.at[z],
+            send_sem=up_line_send_sem.at[offset], recv_sem=up_line_recv_sem.at[offset],
+            device_id=(dp, lax.rem(z + offset, 8) * 4 + x), device_id_type=MESH,
+        )
+
     def all_copy(offset):
         _, device = plane_device(offset)
         return pltpu.make_async_remote_copy(
@@ -324,9 +378,9 @@
     pair_copy(PAIR_PARTS).start()
     for part in range(PAIR_PARTS):
         for piece in range(part * PAIR_PIECES, (part + 1) * PAIR_PIECES):
-            grads = adapter_scale * dot(total_low, hidden_ref[:, piece * PIECE:(piece + 1) * PIECE])
-            down_part[0, piece] = grads[:HALF]
-            down_part[1, piece] = grads[HALF:]
+            for half in range(2):
+                first = half * PIECES * PIECE + piece * PIECE
+                down_part[half, piece] = adapter_scale * dot(total_low, hidden_ref[:, first:first + PIECE])
         pair_copy(part).start()
     pair_copy(PAIR_PARTS).wait_recv()
     up_sum[...] = up_part[core] + up_pair[...]
@@ -334,27 +388,35 @@
         side_copy(offset).start()
     for part in range(PAIR_PARTS):
         pair_copy(part).wait_recv()
-    down_sum[...] = down_part[core] + down_pair[...]
+    down_sum[...] = (down_part[core] + down_pair[...]).astype(BF)
     for offset in range(1, PIECES):
         plane_copy(offset).start()
+    if DEFER:
+        send_context(3)
 
     for offset in range(1, 4):
         side_copy(offset).wait_recv()
-    line_buf[z, :, PIECE:] = ((up_sum[y] + up_recv[1]) + up_recv[2]) + up_recv[3]
-    reduced = down_sum[own_piece]
+    up_line_buf[z] = ((up_sum[y] + up_recv[1]) + up_recv[2]) + up_recv[3]
+    for offset in range(1, 8):
+        up_line_copy(offset).start()
+    reduced = down_part[core, own_piece] + down_pair[own_piece]
     for offset in range(1, PIECES):
         plane_copy(offset).wait_recv()
-        reduced = reduced + down_recv[offset]
-    line_buf[z, :, :PIECE] = reduced
+        reduced = reduced + down_recv[offset].astype(F32)
+    line_buf[z] = reduced.astype(BF)
     for offset in range(1, 8):
         line_copy(offset).start()
     for offset in range(1, 8):
+        up_line_copy(offset).wait_recv()
+    even = (up_line_buf[0] + up_line_buf[2]) + (up_line_buf[4] + up_line_buf[6])
+    odd = (up_line_buf[1] + up_line_buf[3]) + (up_line_buf[5] + up_line_buf[7])
+    all_buf[core, own_piece, 1] = jnp.concatenate([even, odd], axis=0).astype(BF)
+    for offset in range(1, 8):
         line_copy(offset).wait_recv()
-    even = line_buf[0] + line_buf[2] + (line_buf[4] + line_buf[6])
-    odd = line_buf[1] + line_buf[3] + (line_buf[5] + line_buf[7])
-    all_buf[core, own_piece, :, :PIECE] = even[:, :PIECE] + odd[:, :PIECE]
-    all_buf[core, own_piece, :, PIECE:PIECE + HEAD_DIM] = even[:, PIECE:]
-    all_buf[core, own_piece, :, PIECE + HEAD_DIM:] = odd[:, PIECE:]
+    terms = [line_buf[i].astype(F32) for i in range(8)]
+    all_buf[core, own_piece, 0] = (
+        ((terms[0] + terms[1]) + (terms[2] + terms[3])) + ((terms[4] + terms[5]) + (terms[6] + terms[7]))
+    ).astype(BF)
     for offset in range(1, PIECES):
         all_copy(offset).start()
     last_copy(0).start()
@@ -364,22 +426,12 @@
     for offset in range(PIECES):
         last_copy(offset).wait_recv()
 
-    for half in range(2):
-        for piece in range(PIECES):
-            at_y, at_x = piece // 4, piece % 4
-            rows_of = slice(half * HALF, (half + 1) * HALF)
-            grad_down_ref[rows_of, piece * PIECE:(piece + 1) * PIECE] = all_buf[half, piece, :, :PIECE]
-            for parity in range(2):
-                position = (parity if at_y < 2 else 1 - parity) * 4 + at_x
-                grad_up_ref[16 * (at_y // 2) + 2 * position + at_y % 2, rows_of] = all_buf[
-                    half, piece, :, PIECE + parity * HEAD_DIM:PIECE + (parity + 1) * HEAD_DIM
-                ]
-
     def finish(chunk, carry):
         for offset in OFFSETS:
             context_copy(chunk, offset).wait_recv()
             context_copy(chunk, offset).wait_send()
             data_copy(chunk, offset).wait_send()
+        own_context(chunk).wait()
         return carry
 
     lax.fori_loop(0, 4, finish, 0)
@@ -393,6 +445,7 @@
         side_copy(offset).wait_send()
     for offset in range(1, 8):
         line_copy(offset).wait_send()
+        up_line_copy(offset).wait_send()
     for offset in range(PIECES):
         last_copy(offset).wait_send()
         if offset:
@@ -402,13 +455,6 @@
 
 def body(hidden, query, key, value, cotangent, down, up, mask):
     width = hidden.shape[2]
-    order = jnp.arange(HEADS, dtype=jnp.int32)
-    shifted = (mask == 1).astype(jnp.int32)
-    ahead = (order[None, :] < order[:, None]).astype(jnp.int32)
-    shifted_ahead = jnp.sum(ahead * shifted[None, :], axis=1)
-    inverse = jnp.where(shifted == 1, HEADS // 2 + shifted_ahead, order - shifted_ahead)
-    perm = jnp.sum(jnp.where(inverse[None, :] == order[:, None], order[None, :], 0), axis=1)
-
     vmem = pl.BlockSpec(memory_space=pltpu.VMEM)
     smem = pl.BlockSpec(memory_space=pltpu.SMEM)
     dma = pltpu.SemaphoreType.DMA
@@ -426,28 +472,27 @@
                 pl.BlockSpec((MAPS * RANK, TOKENS), lambda i, p: (0, 0)),
                 pl.BlockSpec((4, MAPS * RANK, HEAD_DIM), lambda i, p: (0, 0, 0)),
             ),
-            scratch_shapes=[pltpu.VMEM((TOKENS, MAPS * RANK), BF)],
+            scratch_shapes=[pltpu.VMEM((TOKENS, MAPS * RANK), BF), pltpu.SMEM((HEADS,), jnp.int32)],
         ),
         out_shape=(
             jax.ShapeDtypeStruct((4, MEMBERS, 4 * TOKENS, HEAD_DIM), BF),
             jax.ShapeDtypeStruct((MAPS * RANK, TOKENS), BF),
             jax.ShapeDtypeStruct((4, MAPS * RANK, HEAD_DIM), BF),
         ),
-        compiler_params=pltpu.CompilerParams(vmem_limit_bytes=32 * 1024 * 1024),
+        compiler_params=pltpu.CompilerParams(vmem_limit_bytes=VMEM_GRANT),
         name="project",
     )(
-        perm, hidden[0], query[0], key[0], value[0], cotangent[0],
+        mask, hidden[0], query[0], key[0], value[0], cotangent[0],
         jnp.transpose(down, (0, 2, 1)).reshape(MAPS * RANK, width), up.reshape(MAPS * RANK, width),
     )
-    by_order, grad_down, grad_up = pl.pallas_call(
+    by_order, summed = pl.pallas_call(
         attention_kernel,
         out_shape=(
             jax.ShapeDtypeStruct((HEADS, TOKENS, HEAD_DIM), BF),
-            jax.ShapeDtypeStruct((MAPS * RANK, width), F32),
-            jax.ShapeDtypeStruct((HEADS, MAPS * RANK, HEAD_DIM), F32),
+            jax.ShapeDtypeStruct((2, PIECES, 2, MAPS * RANK, HEAD_DIM), BF),
         ),
         in_specs=[any_space, vmem, vmem, vmem],
-        out_specs=(vmem, vmem, vmem),
+        out_specs=(any_space, vmem),
         scratch_shapes=[
             pltpu.VMEM((4, MEMBERS, 4 * TOKENS, HEAD_DIM), BF),
             pltpu.VMEM((2, MEMBERS, MAPS * RANK, TOKENS), BF),
@@ -460,36 +505,39 @@
             pltpu.VMEM((HEAD_DIM, GROUP), BF),
             pltpu.VMEM((GROUP, HEAD_DIM), F32),
             pltpu.VMEM((GROUP, HEAD_DIM), F32),
-            pltpu.VMEM((2, PIECES, HALF, PIECE), F32),
-            pltpu.VMEM((PIECES, HALF, PIECE), F32),
-            pltpu.VMEM((PIECES, HALF, PIECE), F32),
-            pltpu.VMEM((PIECES, HALF, PIECE), F32),
+            pltpu.VMEM((2, PIECES, MAPS * RANK, PIECE), F32),
+            pltpu.VMEM((PIECES, MAPS * RANK, PIECE), F32),
+            pltpu.VMEM((PIECES, MAPS * RANK, PIECE), BF),
+            pltpu.VMEM((PIECES, MAPS * RANK, PIECE), BF),
             pltpu.VMEM((2, 4, HALF, HEAD_DIM), F32),
             pltpu.VMEM((4, HALF, HEAD_DIM), F32),
             pltpu.VMEM((4, HALF, HEAD_DIM), F32),
             pltpu.VMEM((4, HALF, HEAD_DIM), F32),
-            pltpu.VMEM((8, HALF, PIECE + HEAD_DIM), F32),
-            pltpu.VMEM((2, PIECES, HALF, PIECE + 2 * HEAD_DIM), F32),
+            pltpu.VMEM((8, MAPS * RANK, PIECE), BF),
+            pltpu.VMEM((8, HALF, HEAD_DIM), F32),
             dma((4, MEMBERS)), dma((4, MEMBERS)), dma((2, MEMBERS)), dma((2, MEMBERS)),
             dma((4, MEMBERS)), dma((4, MEMBERS)), dma((2, MEMBERS)), dma((2, MEMBERS)),
             dma((PAIR_PARTS + 1,)), dma((PAIR_PARTS + 1,)), dma((PIECES,)), dma((PIECES,)), dma((4,)), dma((4,)),
-            dma((8,)), dma((8,)), dma((PIECES,)), dma((PIECES,)), dma((PIECES,)), dma((PIECES,)),
+            dma((8,)), dma((8,)), dma((8,)), dma((8,)), dma((4,)), dma((PIECES,)), dma((PIECES,)), dma((PIECES,)), dma((PIECES,)),
         ],
         compiler_params=pltpu.CompilerParams(
-            collective_id=0, has_side_effects=True, vmem_limit_bytes=40 * 1024 * 1024
+            collective_id=0, has_side_effects=True, vmem_limit_bytes=VMEM_GRANT
         ),
         name="shifted_group_attention",
     )(send, low_t, own_up, hidden[0])
-    context, grad_up = pl.pallas_call(
+    context, grad_down, grad_up = pl.pallas_call(
         restore_kernel,
         out_shape=(
             jax.ShapeDtypeStruct((TOKENS, width), BF),
             jax.ShapeDtypeStruct((MAPS * RANK, width), F32),
+            jax.ShapeDtypeStruct((MAPS * RANK, width), F32),
         ),
-        in_specs=[smem, vmem, vmem],
-        out_specs=(vmem, vmem),
+        in_specs=[smem, any_space, vmem],
+        out_specs=(vmem, vmem, vmem),
+        scratch_shapes=[dma((HEADS,))],
+        compiler_params=pltpu.CompilerParams(vmem_limit_bytes=VMEM_GRANT),
         name="restore_heads",
-    )(inverse, by_order, grad_up)
+    )(mask, by_order, summed)
     grad_up = grad_up.reshape(MAPS, RANK, width)
     grad_down = jnp.transpose(grad_down.reshape(MAPS, RANK, width), (0, 2, 1))
     return context[None], grad_down, grad_up

time: 133 us -> 117 us (0.88)
  local copies, waits for them, and re-layouts: 10.8 us -> 0 us
  Pallas kernels: 119 us -> 116 us
  other arithmetic: 1.55 us -> 0 us
    unnamed x23 -> x0, local copies, waits for them, and re-layouts: 10.8 us -> none
    pallas_call x1, Pallas kernels: 113 us -> 103 us  [body(): pl.pallas_call(attention_kernel, out_shape=(jax.ShapeDtypeStruct((HEADS,...]
    pallas_call x1, Pallas kernels: 3.71 us -> 8.73 us  [body(): pl.pallas_call(project_kernel, grid_spec=pltpu.PrefetchScalarGridSpec(num...]
where the time goes in v3:
time: 117 us
  Pallas kernels  116 us (99%)
    pallas_call x1, Pallas kernels, body(): pl.pallas_call(attention_kernel, out_shape=(jax.ShapeDtypeStruct((HEADS,...  103 us
    pallas_call x1, Pallas kernels, body(): pl.pallas_call(project_kernel, grid_spec=pltpu.PrefetchScalarGridSpec(num...  8.73 us
    pallas_call x1, Pallas kernels, body(): pl.pallas_call(restore_kernel, out_shape=(jax.ShapeDtypeStruct((TOKENS, w...  4.19 us

profile of v3, /device:TPU:1, one launch (start us, length us, event | category | flops | bytes accessed | tf_op | source)
XLA Modules:
  0.0 116.6 jit_solution(11296556349300274902)
XLA Ops:
  0.6 8.7 %project.1 = (bf16[4,8,512,128]{3,2,1,0:T(8,128)(2,1)}, bf16[48,128]{1,0:T(8,128)(2,1)}, bf16[4,48,128]{2,1,0:T(8,128)(2,1)}) custom-call(s32[32]{0:T(128)} %mask_ref.3, bf16[128,4096]{1,0:T(8,128)(2,1)} %bitcast.14, bf16[128,4096]{1,0:T(8,128)(2,1)} %bitcast.16, bf16[128,4096]{1,0:T(8,128)(2,1)} %bitcast.17, bf16[128,4096]{1,0:T(8,128)(2,1)} %bitcast.18, ...), custom_call_target="tpu_custom_call" | custom-call | tf_op jit(solution)/shard_map/project/pallas_call | solution.py:464
  9.4 103.0 %shifted_group_attention.1 = (bf16[32,128,128]{2,1,0:T(8,128)(2,1)}, bf16[2,16,2,48,128]{4,3,2,1,0:T(8,128)(2,1)}) custom-call(bf16[4,8,512,128]{3,2,1,0:T(8,128)(2,1)} %get-tuple-element.11.send_buf, bf16[48,128]{1,0:T(8,128)(2,1)} %get-tuple-element.12.low_own, bf16[4,48,128]{2,1,0:T(8,128)(2,1)} %get-tuple-element.13.own_up, bf16[128,4096]{1,0:T(8,128)(2,1)} %bitcast.15), custom_call_target="tpu_custom_call" | custom-call | tf_op jit(solution)/shard_map/shifted_group_attention/pallas_call | solution.py:488
  112.4 4.2 %restore_heads.1 = (bf16[128,4096]{1,0:T(8,128)(2,1)}, f32[48,4096]{1,0:T(8,128)}, f32[48,4096]{1,0:T(8,128)}) custom-call(s32[32]{0:T(128)} %mask_ref.3, bf16[32,128,128]{2,1,0:T(8,128)(2,1)} %get-tuple-element.14.by_order_ref, bf16[2,16,2,48,128]{4,3,2,1,0:T(8,128)(2,1)} %get-tuple-element.15.all_ref), custom_call_target="tpu_custom_call" | custom-call | tf_op jit(solution)/shard_map/restore_heads/pallas_call | solution.py:528
